TPU v7x, 32 devices: a whole 2x2x4 slice. The times are simulated.
32 devices in a mesh: dp: 8 (over y, x, core), tensor: 4 (over z).
Axes of the slice: x: 2, y: 2, z: 4, core: 2. Of those that a mesh axis runs over, the one named last changes fastest.
Arguments:
- images: bfloat16 [64, 257, 1664], P(('dp', 'tensor')), may hold values from -6 to 6
- first_gain: float32 [1664], replicated, may hold values from 0.5 to 1.5
- first_shift: float32 [1664], replicated, may hold values from -4 to 4
- qkv_weight: bfloat16 [3, 1664, 1664], P(None, None, 'tensor'), as said below
- qv_bias: float32 [2, 1664], P(None, 'tensor'), may hold values from -6 to 6
- out_weight: bfloat16 [1664, 1664], P('tensor'), may hold values from -0.625 to 0.625
- out_bias: float32 [1664], replicated, may hold values from -4 to 4
- second_gain: float32 [1664], replicated, may hold values from 0.5 to 1.5
- second_shift: float32 [1664], replicated, may hold values from -4 to 4
- up_weight: bfloat16 [1664, 8192], P(None, 'tensor'), may hold values from -0.15625 to 0.15625
- up_bias: float32 [8192], P('tensor'), may hold values from -6 to 6
- down_weight: bfloat16 [8192, 1664], P('tensor'), may hold values from -0.0625 to 0.0625
- down_bias: float32 [1664], replicated, may hold values from -4 to 4
- cotangent: bfloat16 [64, 257, 1664], P(('dp', 'tensor')), may hold values from -6 to 6
Outputs:
- result: bfloat16 [64, 257, 1664], P(('dp', 'tensor'))
- grad_images: bfloat16 [64, 257, 1664], P(('dp', 'tensor'))
- grad_first_gain: float32 [1664], replicated
- grad_first_shift: float32 [1664], replicated
- grad_qkv_weight: float32 [3, 1664, 1664], P(None, None, 'tensor')
- grad_qv_bias: float32 [2, 1664], P(None, 'tensor')
- grad_out_weight: float32 [1664, 1664], P('tensor')
- grad_out_bias: float32 [1664], replicated
- grad_second_gain: float32 [1664], replicated
- grad_second_shift: float32 [1664], replicated
- grad_up_weight: float32 [1664, 8192], P(None, 'tensor')
- grad_up_bias: float32 [8192], P('tensor')
- grad_down_weight: float32 [8192, 1664], P('tensor')
- grad_down_bias: float32 [1664], replicated
Inputs may be any that keep to these rules, and one draw needn't show every extreme that they name: `qkv_weight`: the three parts are query, keys and values, in this order.
All inputs are finite; a program needn't handle non-finite values.
Results may differ from a plain program's by a relative error of at most 0.02.
Values may be sent and summed in bfloat16 or wider, within the bound.
A program may use at most 256 MiB of HBM per device.

v0:
```python
import jax
import jax.numpy as jnp
from jax import lax
from jax.sharding import PartitionSpec as P

HD = 104
epsilon = 1e-06
inv_root_two = 0.7071067811865476
inv_root_tau = 0.3989422804014327


def normalize(rows):
    centre = jnp.mean(rows, axis=-1, keepdims=True)
    centred = rows - centre
    spread = jnp.mean(centred * centred, axis=-1, keepdims=True)
    inverse = lax.rsqrt(spread + epsilon)
    return (centred * inverse, inverse)


def norm_back(grad, unit, inverse, gain):
    scaled = grad * gain
    first = jnp.mean(scaled, axis=-1, keepdims=True)
    second = jnp.mean(scaled * unit, axis=-1, keepdims=True)
    return inverse * (scaled - first - unit * second)


def attend_block(query, keys, values):
    factor = query.shape[-1] ** (-0.5)
    scores = jnp.einsum("bshd,bthd->bhst", query, keys, preferred_element_type=jnp.float32) * factor
    top = jnp.max(scores, axis=-1, keepdims=True)
    raised = jnp.exp(scores - top)
    total = jnp.sum(raised, axis=-1, keepdims=True)
    weights = (raised / total).astype(jnp.bfloat16)
    mixed = jnp.einsum("bhst,bthd->bshd", weights, values, preferred_element_type=jnp.float32)
    return (mixed, (top + jnp.log(total))[..., 0])


def attend_back(query, keys, values, grad_out, log_total):
    factor = query.shape[-1] ** (-0.5)
    scores = jnp.einsum("bshd,bthd->bhst", query, keys, preferred_element_type=jnp.float32) * factor
    probs = jnp.exp(scores - log_total[..., None])
    grad_values = jnp.einsum(
        "bhst,bshd->bthd", probs.astype(jnp.bfloat16), grad_out, preferred_element_type=jnp.float32
    )
    grad_probs = jnp.einsum("bshd,bthd->bhst", grad_out, values, preferred_element_type=jnp.float32)
    inner = jnp.sum(probs * grad_probs, axis=-1, keepdims=True)
    grad_scores = (probs * (grad_probs - inner)).astype(jnp.bfloat16)
    grad_query = (
        jnp.einsum("bhst,bthd->bshd", grad_scores, keys, preferred_element_type=jnp.float32)
        * factor
    )
    grad_keys = (
        jnp.einsum("bhst,bshd->bthd", grad_scores, query, preferred_element_type=jnp.float32)
        * factor
    )
    return (
        grad_query.astype(jnp.bfloat16),
        grad_keys.astype(jnp.bfloat16),
        grad_values.astype(jnp.bfloat16),
    )


def on_device(
    images,
    first_gain,
    first_shift,
    qkv_weight,
    qv_bias,
    out_weight,
    out_bias,
    second_gain,
    second_shift,
    up_weight,
    up_bias,
    down_weight,
    down_bias,
    cotangent,
):
    seq_len = images.shape[1]
    columns = qkv_weight.shape[2]
    heads_here = columns // HD
    inputs = images.astype(jnp.float32)
    unit_first, inverse_first = normalize(inputs)
    normed_local = (unit_first * first_gain + first_shift).astype(jnp.bfloat16)
    normed_first = lax.all_gather(normed_local, "tensor", axis=0, tiled=True)
    count = normed_first.shape[0]
    projected = jnp.einsum(
        "isd,nde->nise", normed_first, qkv_weight, preferred_element_type=jnp.float32
    )
    query = (projected[0] + qv_bias[0]).astype(jnp.bfloat16)
    keys = projected[1].astype(jnp.bfloat16)
    values = (projected[2] + qv_bias[1]).astype(jnp.bfloat16)
    split = (count // 2, 2, seq_len, heads_here, HD)
    query_blocks = query.reshape(split)
    key_blocks = keys.reshape(split)
    value_blocks = values.reshape(split)
    mixed, log_total = lax.map(
        lambda triple: attend_block(triple[0], triple[1], triple[2]),
        (query_blocks, key_blocks, value_blocks),
    )
    heads_out = mixed.reshape(count, seq_len, columns).astype(jnp.bfloat16)
    piece = heads_out
    attention = lax.psum_scatter(
        jnp.einsum("isc,cd->isd", piece, out_weight, preferred_element_type=jnp.float32).astype(
            jnp.bfloat16
        ),
        "tensor",
        scatter_dimension=0,
        tiled=True,
    ).astype(jnp.float32)
    middle = inputs + (attention + out_bias)
    unit_second, inverse_second = normalize(middle)
    normed_second = lax.all_gather(
        (unit_second * second_gain + second_shift).astype(jnp.bfloat16),
        "tensor",
        axis=0,
        tiled=True,
    )
    hidden = (
        jnp.einsum("isd,df->isf", normed_second, up_weight, preferred_element_type=jnp.float32)
        + up_bias
    )
    active = jax.nn.gelu(hidden, approximate=False).astype(jnp.bfloat16)
    piece = active
    result = (
        middle
        + lax.psum_scatter(
            jnp.einsum(
                "isf,fd->isd", piece, down_weight, preferred_element_type=jnp.float32
            ).astype(jnp.bfloat16),
            "tensor",
            scatter_dimension=0,
            tiled=True,
        ).astype(jnp.float32)
        + down_bias
    ).astype(jnp.bfloat16)
    seed_rows = lax.all_gather(cotangent, "tensor", axis=0, tiled=True)
    grad_down_weight = jnp.einsum(
        "isf,isd->fd", active, seed_rows, preferred_element_type=jnp.float32
    )
    grad_down_bias = jnp.sum(cotangent, axis=(0, 1), dtype=jnp.float32)
    grad_active = jnp.einsum(
        "isd,fd->isf", seed_rows, down_weight, preferred_element_type=jnp.float32
    )
    normal_cdf = 0.5 * (1.0 + lax.erf(hidden * inv_root_two))
    density = jnp.exp(-0.5 * hidden * hidden) * inv_root_tau
    grad_hidden = (grad_active * (normal_cdf + hidden * density)).astype(jnp.bfloat16)
    grad_up_weight = jnp.einsum(
        "isd,isf->df", normed_second, grad_hidden, preferred_element_type=jnp.float32
    )
    grad_up_bias = jnp.sum(grad_hidden, axis=(0, 1), dtype=jnp.float32)
    piece = grad_hidden
    grad_normed_second = lax.psum_scatter(
        jnp.einsum("isf,df->isd", piece, up_weight, preferred_element_type=jnp.float32).astype(
            jnp.bfloat16
        ),
        "tensor",
        scatter_dimension=0,
        tiled=True,
    ).astype(jnp.float32)
    grad_second_gain = jnp.sum(grad_normed_second * unit_second, axis=(0, 1))
    grad_second_shift = jnp.sum(grad_normed_second, axis=(0, 1))
    grad_middle = cotangent.astype(jnp.float32) + norm_back(
        grad_normed_second, unit_second, inverse_second, second_gain
    )
    grad_branch = grad_middle.astype(jnp.bfloat16)
    grad_out_bias = jnp.sum(grad_branch, axis=(0, 1), dtype=jnp.float32)
    branch_rows = lax.all_gather(grad_branch, "tensor", axis=0, tiled=True)
    grad_out_weight = jnp.einsum(
        "isc,isd->cd", heads_out, branch_rows, preferred_element_type=jnp.float32
    )
    grad_heads = jnp.einsum(
        "isd,cd->isc", branch_rows, out_weight, preferred_element_type=jnp.float32
    ).astype(jnp.bfloat16)
    grad_query, grad_keys, grad_values = lax.map(
        lambda parts: attend_back(parts[0], parts[1], parts[2], parts[3], parts[4]),
        (query_blocks, key_blocks, value_blocks, grad_heads.reshape(split), log_total),
    )
    grad_projected = jnp.stack(
        [
            grad_query.reshape(count, seq_len, columns),
            grad_keys.reshape(count, seq_len, columns),
            grad_values.reshape(count, seq_len, columns),
        ]
    )
    grad_qkv_weight = jnp.einsum(
        "isd,nisc->ndc", normed_first, grad_projected, preferred_element_type=jnp.float32
    )
    grad_qv_bias = jnp.stack(
        [
            jnp.sum(grad_projected[0], axis=(0, 1), dtype=jnp.float32),
            jnp.sum(grad_projected[2], axis=(0, 1), dtype=jnp.float32),
        ]
    )
    piece = grad_projected
    grad_normed_first = lax.psum_scatter(
        jnp.einsum("nisc,ndc->isd", piece, qkv_weight, preferred_element_type=jnp.float32).astype(
            jnp.bfloat16
        ),
        "tensor",
        scatter_dimension=0,
        tiled=True,
    ).astype(jnp.float32)
    grad_first_gain = jnp.sum(grad_normed_first * unit_first, axis=(0, 1))
    grad_first_shift = jnp.sum(grad_normed_first, axis=(0, 1))
    grad_images = (
        grad_middle + norm_back(grad_normed_first, unit_first, inverse_first, first_gain)
    ).astype(jnp.bfloat16)
    (
        grad_qkv_weight,
        grad_qv_bias,
        grad_out_weight,
        grad_up_weight,
        grad_up_bias,
        grad_down_weight,
    ) = (
        lax.psum(grad_qkv_weight.astype(jnp.bfloat16), "dp").astype(jnp.float32),
        lax.psum(grad_qv_bias.astype(jnp.bfloat16), "dp").astype(jnp.float32),
        lax.psum(grad_out_weight.astype(jnp.bfloat16), "dp").astype(jnp.float32),
        lax.psum(grad_up_weight.astype(jnp.bfloat16), "dp").astype(jnp.float32),
        lax.psum(grad_up_bias.astype(jnp.bfloat16), "dp").astype(jnp.float32),
        lax.psum(grad_down_weight.astype(jnp.bfloat16), "dp").astype(jnp.float32),
    )
    (
        grad_first_gain,
        grad_first_shift,
        grad_out_bias,
        grad_second_gain,
        grad_second_shift,
        grad_down_bias,
    ) = lax.psum(
        (
            grad_first_gain,
            grad_first_shift,
            grad_out_bias,
            grad_second_gain,
            grad_second_shift,
            grad_down_bias,
        ),
        ("dp", "tensor"),
    )
    return (
        result,
        grad_images,
        grad_first_gain,
        grad_first_shift,
        grad_qkv_weight,
        grad_qv_bias,
        grad_out_weight,
        grad_out_bias,
        grad_second_gain,
        grad_second_shift,
        grad_up_weight,
        grad_up_bias,
        grad_down_weight,
        grad_down_bias,
    )


def solution(mesh):
    return jax.shard_map(
        on_device,
        mesh=mesh,
        in_specs=(
            P(("dp", "tensor"), None, None),
            P(),
            P(),
            P(None, None, "tensor"),
            P(None, "tensor"),
            P("tensor", None),
            P(),
            P(),
            P(),
            P(None, "tensor"),
            P("tensor"),
            P("tensor", None),
            P(),
            P(("dp", "tensor"), None, None),
        ),
        out_specs=(
            P(("dp", "tensor"), None, None),
            P(("dp", "tensor"), None, None),
            P(),
            P(),
            P(None, None, "tensor"),
            P(None, "tensor"),
            P("tensor", None),
            P(),
            P(),
            P(),
            P(None, "tensor"),
            P("tensor"),
            P("tensor", None),
            P(),
        ),
        check_vma=False,
    )
```

profile of v0, /device:TPU:0, one launch (start us, length us, event | category | flops | bytes accessed | tf_op | source)
XLA Modules:
  0.0 1597.7 jit_solution(3615522905375342727)
XLA Ops:
  14.7 130.0 %all-gather.5.cloned.1.call-done = bf16[8,257,1664]{2,1,0:T(8,128)(2,1)} async-done(((bf16[2,257,1664]{2,1,0:T(8,128)(2,1)}), bf16[8,257,1664]{2,1,0:T(8,128)(2,1)}) %all-gather.5.cloned.1.call-update) | async-done | bytes 6842384 | tf_op jit(solution)/shard_map/all_gather | solution.py:85
  144.7 15.5 convolution_bitcast_fusion
  196.2 24.4 %while.26 = (s32[]{:T(128)}, bf16[4,2,257,4,104]{4,2,3,1,0:T(8,128)(2,1)}, f32[4,2,4,257]{3,2,1,0:T(4,128)}, bf16[4,2,257,4,104]{4,2,3,1,0:T(8,128)(2,1)}, bf16[...) while((s32[]{:T(128)}, bf16[4,2,257,4,104]{4,2,3,1,0:T(8,128)(2,1)}, ...), condition=%wide.region_5.6_spmd, body=%wide.region_2.5_spmd.sunk | while | flops 224564544 | bytes 9116557 | solution.py:97
  237.2 121.2 %reduce-scatter.5.cloned.1.call-done = bf16[2,257,1664]{2,1,0:T(8,128)(2,1)} async-done(((bf16[8,257,1664]{2,1,0:T(8,128)(2,1)}), bf16[2,257,1664]{2,1,0:T(8,128)(2,1)}) %reduce-scatter.5.cloned.1.call-update) | async-done | bytes 1710608 | tf_op jit(solution)/shard_map/reduce_scatter | solution.py:103
  366.6 125.1 %all-gather.7.cloned.1.call-done = bf16[8,257,1664]{2,1,0:T(8,128)(2,1)} async-done(((bf16[2,257,1664]{2,1,0:T(8,128)(2,1)}), bf16[8,257,1664]{2,1,0:T(8,128)(2,1)}) %all-gather.7.cloned.1.call-update) | async-done | bytes 6842384 | tf_op jit(solution)/shard_map/all_gather | solution.py:113
  491.7 28.5 %fusion.91 = (u8[257,2048]{1,0:T(8,128)(4,1)}, u8[257,2048]{1,0:T(8,128)(4,1)}, f32[8,257,2048]{2,1,0:T(8,128)}) fusion(f32[2048]{0:T(1024)S(1)} %copy-done.39, bf16[8,257,1664]{2,1,0:T(8,128)(2,1)} %all-gather.7.cloned.1.call-done, bf16[1664,2048]{1,0:T(8,128)(2,1)} %param.27), kind=kOutput, calls=%fused_computation.123 | convolution fusion | flops 14071066624 | bytes 31561728 | tf_op jit(solution)/shard_map/isd,df->isf/dot_general | solution.py:120
  520.2 99.3 %all-gather.9.cloned.1.call-done = bf16[8,257,1664]{2,1,0:T(8,128)(2,1)} async-done(((bf16[2,257,1664]{2,1,0:T(8,128)(2,1)}), bf16[8,257,1664]{2,1,0:T(8,128)(2,1)}) %all-gather.9.cloned.1.call-update) | async-done | bytes 6842384 | tf_op jit(solution)/shard_map/all_gather | solution.py:137
  619.5 29.1 %fusion.123 = (bf16[2048]{0:T(1024)(128)(2,1)}, bf16[8,257,2048]{2,1,0:T(8,128)(2,1)S(1)}) fusion(f32[8,257,2048]{2,1,0:T(8,128)} %get-tuple-element.253, f32[2048]{0:T(1024)S(1)} %copy-done.39, bf16[8,257,1664]{2,1,0:T(8,128)(2,1)} %all-gather.9.cloned.1.call-done, bf16[2048,1664]{1,0:T(8,128)(2,1)} %param.29), kind=kOutput, calls=%fused_computation.175 | convolution fusion | flops 14063695872 | bytes 38934528 | tf_op jit(solution)/shard_map/isd,fd->isf/dot_general | solution.py:142
  652.1 21.0 %fusion.78 = bf16[8,257,1664]{2,1,0:T(8,128)(2,1)} fusion(bf16[8,257,2048]{2,1,0:T(8,128)(2,1)S(1)} %get-tuple-element.255, bf16[1664,2048]{1,0:T(8,128)(2,1)} %param.27), kind=kOutput, calls=%fused_computation.102 | convolution fusion | flops 14016590848 | bytes 22079488 | tf_op jit(solution)/shard_map/isf,df->isd/dot_general | solution.py:154
  673.2 121.2 %reduce-scatter.9.cloned.1.call-done = bf16[2,257,1664]{2,1,0:T(8,128)(2,1)} async-done(((bf16[8,257,1664]{2,1,0:T(8,128)(2,1)}), bf16[2,257,1664]{2,1,0:T(8,128)(2,1)}) %reduce-scatter.9.cloned.1.call-update) | async-done | bytes 1710608 | tf_op jit(solution)/shard_map/reduce_scatter | solution.py:153
  802.8 42.3 %fusion.52 = bf16[8,257,2048]{2,1,0:T(8,128)(2,1)S(1)} fusion(f32[8,257,2048]{2,1,0:T(8,128)} %get-tuple-element.253, f32[2048]{0:T(1024)S(1)} %copy-done.39, u8[257,2048]{1,0:T(8,128)(4,1)} %get-tuple-element.189, u8[257,2048]{1,0:T(8,128)(4,1)} %get-tuple-element.188), kind=kLoop, calls=%fused_computation.60 | loop fusion | flops 298958848 | bytes 26324992 | tf_op jit(solution)/shard_map/convert_element_type | solution.py:123
  845.2 25.8 %bitcast_convert_fusion.1 = bf16[2048,1664]{1,0:T(8,128)(2,1)} fusion(bf16[8,257,2048]{2,1,0:T(8,128)(2,1)S(1)} %fusion.52, bf16[8,257,1664]{2,1,0:T(8,128)(2,1)} %all-gather.9.cloned.1.call-done), kind=kOutput, calls=%fused_computation.86 | convolution fusion | flops 14016577536 | bytes 22079488 | tf_op jit(solution)/shard_map/isf,isd->fd/dot_general | solution.py:138
  871.1 18.5 %bitcast_convert_fusion.2 = bf16[1664,2048]{1,0:T(8,128)(2,1)} fusion(bf16[8,257,1664]{2,1,0:T(8,128)(2,1)S(1)} %bitcast.177, bf16[8,257,2048]{2,1,0:T(8,128)(2,1)S(1)} %bitcast.179), kind=kOutput, calls=%fused_computation.87 | convolution fusion | flops 14016577536 | bytes 22079488 | tf_op jit(solution)/shard_map/isd,isf->df/dot_general | solution.py:148
  889.5 41.3 %all-gather.11.cloned.1.call-done = bf16[8,257,1664]{2,1,0:T(8,128)(2,1)} async-done(((bf16[2,257,1664]{2,1,0:T(8,128)(2,1)}), bf16[8,257,1664]{2,1,0:T(8,128)(2,1)}) %all-gather.11.cloned.1.call-update) | async-done | bytes 6842384 | tf_op jit(solution)/shard_map/all_gather | solution.py:168
  944.1 50.2 %while.27 = (s32[]{:T(128)}, bf16[4,2,257,4,104]{4,2,3,1,0:T(8,128)(2,1)}, bf16[4,2,257,4,104]{4,3,2,1,0:T(4,128)(2,1)}, bf16[4,2,257,4,104]{4,2,3,1,0:T(8,128)(...) while((s32[]{:T(128)}, ...), condition=%wide.region_15.16_spmd, body=%wide.region_13.15_spmd.sunk | while | flops 556935424 | bytes 23355692 | solution.py:175
  1026.3 15.7 fusion.98
  1042.1 15.3 bitcast_convert_fusion
  1057.5 21.5 %fusion.81 = bf16[8,257,1664]{2,1,0:T(8,128)(2,1)} fusion(bf16[8,257,2048]{2,1,0:T(8,128)(2,1)} %copy-done.9, bf16[2048,1664]{1,0:T(8,128)(2,1)} %param.29), kind=kOutput, calls=%fused_computation.103 | convolution fusion | flops 14016590848 | bytes 22079488 | tf_op jit(solution)/shard_map/isf,fd->isd/dot_general | solution.py:128
  1083.3 15.5 all-reduce.1
  1100.1 186.1 %all-reduce.5.cloned.1.call-done = (bf16[3,1664,416]{1,2,0:T(8,128)(2,1)}, bf16[416,1664]{1,0:T(8,128)(2,1)}, bf16[1664,2048]{1,0:T(8,128)(2,1)}, bf16[2048,1664]{1,0:T(8,128)(2,1)}) async-done(((bf16[3,1664,416]{1,2,0:T(8,128)(2,1)}, bf16[416,1664]{1,0:T(8,128)(2,1)}, bf16[1664,2048]{1,0:T(8,128)(2,1)}, bf16[2048,1664]{1,0:T(8,128)(2,1)}), (bf16[3,1664,416]{1,2,0:T(8,128)(2,1)}, ...) | async-done | bytes 19169296 | tf_op jit(solution)/shard_map/psum | solution.py:217
  1286.1 10.6 convert_element_type.181
  1308.4 102.9 %reduce-scatter.11.cloned.1.call-done = bf16[2,257,1664]{2,1,0:T(8,128)(2,1)} async-done(((bf16[8,257,1664]{2,1,0:T(8,128)(2,1)}), bf16[2,257,1664]{2,1,0:T(8,128)(2,1)}) %reduce-scatter.11.cloned.1.call-update) | async-done | bytes 1710608 | tf_op jit(solution)/shard_map/reduce_scatter | solution.py:196
  1414.4 122.8 %reduce-scatter.7.cloned.1.call-done = bf16[2,257,1664]{2,1,0:T(8,128)(2,1)} async-done(((bf16[8,257,1664]{2,1,0:T(8,128)(2,1)}), bf16[2,257,1664]{2,1,0:T(8,128)(2,1)}) %reduce-scatter.7.cloned.1.call-update) | async-done | bytes 1710608 | tf_op jit(solution)/shard_map/reduce_scatter | solution.py:127
  1548.9 42.1 %all-reduce = (f32[1664]{0:T(1024)}, f32[1664]{0:T(1024)}, f32[1664]{0:T(1024)}, f32[1664]{0:T(1024)}, f32[1664]{0:T(1024)}, /*index=5*/f32[1664]{0:T(1024)}) all-reduce(f32[1664]{0:T(1024)S(1)} %get-tuple-element.192, f32[1664]{0:T(1024)S(1)} %get-tuple-element.197, ...), channel_id=1, replica_groups=mesh['dp'=8,'tensor'=4] {'dp','tensor'}, use_global_device_ids=true, to_apply=%region_20.21 | all-reduce | flops 9984 | bytes 79872 | tf_op jit(solution)/shard_map/psum | solution.py:231
  (232 shorter events, 231.6 us)
Async XLA Ops:
  7.2 221.7 %copy-start = (bf16[416,1664]{1,0:T(8,128)(2,1)S(1)}, bf16[416,1664]{1,0:T(8,128)(2,1)}, u32[]{:S(2)}) copy-start(bf16[416,1664]{1,0:T(8,128)(2,1)} %param.23) | copy-start | bytes 4153348
  7.2 137.5 %all-gather.5.cloned.1.call-start = ((), (), s32[]{:S(2)}) async-start(), calls=%async_computation.4 | async-start | bytes 8785920 | tf_op jit(solution)/shard_map/all_gather | solution.py:85
  14.5 343.9 %reduce-scatter.5.cloned.1.call-start = ((), (), s32[]{:S(2)}) async-start(), calls=%async_computation.5 | async-start | bytes 8785920 | tf_op jit(solution)/shard_map/reduce_scatter | solution.py:103
  237.1 121.3 %copy-start.17 = (f32[1664]{0:T(1024)S(1)}, f32[1664]{0:T(1024)}, u32[]{:S(2)}) copy-start(f32[1664]{0:T(1024)} %param.24) | copy-start | bytes 19972
  237.1 124.3 %copy-start.19 = (f32[1664]{0:T(1024)S(1)}, f32[1664]{0:T(1024)}, u32[]{:S(2)}) copy-start(f32[1664]{0:T(1024)} %param.25) | copy-start | bytes 19972
  237.1 124.3 %copy-start.38 = (f32[1664]{0:T(1024)S(1)}, f32[1664]{0:T(1024)}, u32[]{:S(2)}) copy-start(f32[1664]{0:T(1024)} %param.26) | copy-start | bytes 19972
  237.1 254.6 %all-gather.7.cloned.1.call-start = ((), (), s32[]{:S(2)}) async-start(), calls=%async_computation.6 | async-start | bytes 8785920 | tf_op jit(solution)/shard_map/all_gather | solution.py:113
  360.5 438.2 %copy-start.21 = (f32[2,257]{1,0:T(2,128)}, f32[2,257]{1,0:T(2,128)S(1)}, u32[]{:S(2)}) copy-start(f32[2,257]{1,0:T(2,128)S(1)} %broadcast_multiply_fusion.4) | copy-start | bytes 6172
  361.4 437.2 %copy-start.23 = (f32[2,257]{1,0:T(2,128)}, f32[2,257]{1,0:T(2,128)S(1)}, u32[]{:S(2)}) copy-start(f32[2,257]{1,0:T(2,128)S(1)} %add_rsqrt_fusion) | copy-start | bytes 6172
  363.6 128.1 %copy-start.39 = (f32[2048]{0:T(1024)S(1)}, f32[2048]{0:T(1024)}, u32[]{:S(2)}) copy-start(f32[2048]{0:T(1024)} %param.28) | copy-start | bytes 24580
  363.7 255.8 %all-gather.9.cloned.1.call-start = ((), (), s32[]{:S(2)}) async-start(), calls=%async_computation.8 | async-start | bytes 8785920 | tf_op jit(solution)/shard_map/all_gather | solution.py:137
  366.6 427.8 %reduce-scatter.9.cloned.1.call-start = ((), (), s32[]{:S(2)}) async-start(), calls=%async_computation.9 | async-start | bytes 8785920 | tf_op jit(solution)/shard_map/reduce_scatter | solution.py:153
  673.1 257.8 %all-gather.11.cloned.1.call-start = ((), (), s32[]{:S(2)}) async-start(), calls=%async_computation.10 | async-start | bytes 8785920 | tf_op jit(solution)/shard_map/all_gather | solution.py:168
  802.7 483.4 %all-reduce.5.cloned.1.call-start = ((), (), s32[]{:S(2)}) async-start(), calls=%async_computation.12 | async-start | bytes 38338560 | tf_op jit(solution)/shard_map/psum | solution.py:217
  1042.0 369.3 %reduce-scatter.11.cloned.1.call-start = ((), (), s32[]{:S(2)}) async-start(), calls=%async_computation.11 | async-start | bytes 8785920 | tf_op jit(solution)/shard_map/reduce_scatter | solution.py:196
  1057.4 479.8 %reduce-scatter.7.cloned.1.call-start = ((), (), s32[]{:S(2)}) async-start(), calls=%async_computation.7 | async-start | bytes 8785920 | tf_op jit(solution)/shard_map/reduce_scatter | solution.py:127
  1306.6 104.7 %copy-start.29 = (f32[2,257]{1,0:T(2,128)S(1)}, f32[2,257]{1,0:T(2,128)}, u32[]{:S(2)}) copy-start(f32[2,257]{1,0:T(2,128)} %copy-done.28) | copy-start | bytes 6172
  1306.6 230.6 %copy-start.18 = (f32[1664]{0:T(1024)S(1)}, f32[1664]{0:T(1024)}, u32[]{:S(2)}) copy-start(f32[1664]{0:T(1024)} %param.24) | copy-start | bytes 19972
  1306.7 230.6 %copy-start.20 = (f32[1664]{0:T(1024)S(1)}, f32[1664]{0:T(1024)}, u32[]{:S(2)}) copy-start(f32[1664]{0:T(1024)} %param.25) | copy-start | bytes 19972
  1306.7 230.5 %copy-start.22 = (f32[2,257]{1,0:T(2,128)S(1)}, f32[2,257]{1,0:T(2,128)}, u32[]{:S(2)}) copy-start(f32[2,257]{1,0:T(2,128)} %copy-done.21) | copy-start | bytes 6172
  1306.7 230.5 %copy-start.24 = (f32[2,257]{1,0:T(2,128)S(1)}, f32[2,257]{1,0:T(2,128)}, u32[]{:S(2)}) copy-start(f32[2,257]{1,0:T(2,128)} %copy-done.23) | copy-start | bytes 6172
  1306.7 230.5 %copy-start.35 = (f32[2,257]{1,0:T(2,128)S(1)}, f32[2,257]{1,0:T(2,128)}, u32[]{:S(2)}) copy-start(f32[2,257]{1,0:T(2,128)} %copy-done.34) | copy-start | bytes 6172
  1306.7 230.5 %copy-start.37 = (f32[2,257]{1,0:T(2,128)S(1)}, f32[2,257]{1,0:T(2,128)}, u32[]{:S(2)}) copy-start(f32[2,257]{1,0:T(2,128)} %copy-done.36) | copy-start | bytes 6172
  1306.7 230.5 %copy-start.40 = (f32[1664]{0:T(1024)S(1)}, f32[1664]{0:T(1024)}, u32[]{:S(2)}) copy-start(f32[1664]{0:T(1024)} %param.30) | copy-start | bytes 19972
  (34 other events, 711.5 us)
Sparse Core Ops, SparseCore 0:
  14.6 130.0 all-gather.4
  237.2 121.0 reduce-scatter.4
  363.8 127.9 all-gather.6
  493.8 125.6 all-gather.8
  673.2 121.0 reduce-scatter.8
  802.9 127.9 all-gather.10
  1042.1 243.9 all-reduce.4
  1288.4 122.8 reduce-scatter.10
  1413.8 123.3 reduce-scatter.6
where the time goes:
time: 1610 us; the launch traced here: 1600 us
  waiting for transfers between devices  1050 us (65%)
  matrix products  270 us (17%)
  other arithmetic  112 us (7%)
  local copies, waits for them, and re-layouts  93.3 us (6%)
  blocking collectives  57.6 us (4%)
    psum x1, waiting for transfers between devices, on_device(): lax.psum(grad_qkv_weight.astype(jnp.bfloat16), 'dp').astype(jnp.float32)  186 us
    all_gather x1, waiting for transfers between devices, on_device(): normed_first = lax.all_gather(normed_local, 'tensor', axis=0, tiled=True)  130 us
    all_gather x1, waiting for transfers between devices, on_device(): lax.all_gather((unit_second * second_gain + second_shift).astype(jnp.bflo...  125 us
    reduce_scatter x1, waiting for transfers between devices, on_device(): lax.psum_scatter(jnp.einsum('isf,fd->isd', piece, down_weight, preferred_...  123 us
    reduce_scatter x1, waiting for transfers between devices, on_device(): lax.psum_scatter(jnp.einsum('isc,cd->isd', piece, out_weight, preferred_e...  121 us
    reduce_scatter x1, waiting for transfers between devices, on_device(): lax.psum_scatter(jnp.einsum('isf,df->isd', piece, up_weight, preferred_el...  121 us
    reduce_scatter x1, waiting for transfers between devices, on_device(): lax.psum_scatter(jnp.einsum('nisc,ndc->isd', piece, qkv_weight, preferred...  103 us
    all_gather x1, waiting for transfers between devices, on_device(): seed_rows = lax.all_gather(cotangent, 'tensor', axis=0, tiled=True)  99.3 us
  transfers between devices with their start and end apart: 9, of which 9 were waited for; matrix products, arithmetic and copies ran while one was open for 12% of the time, Pallas kernels for 0%

commit v1 on v0

--- a/solution.py
+++ b/solution.py
@@ -229,15 +229,18 @@
         grad_second_shift,
         grad_down_bias,
     ) = lax.psum(
-        (
-            grad_first_gain,
-            grad_first_shift,
-            grad_out_bias,
-            grad_second_gain,
-            grad_second_shift,
-            grad_down_bias,
-        ),
-        ("dp", "tensor"),
+        lax.psum(
+            (
+                grad_first_gain,
+                grad_first_shift,
+                grad_out_bias,
+                grad_second_gain,
+                grad_second_shift,
+                grad_down_bias,
+            ),
+            "tensor",
+        ),
+        "dp",
     )
     return (
         result,

time: 1610 us -> 1610 us (level)
    psum x0 -> x1, blocking collectives: none -> 23.5 us  [on_device(): lax.psum(lax.psum((grad_first_gain, grad_first_shift, grad_out_bias, grad...]
    psum x1, blocking collectives: 42.1 us -> 18.7 us  [on_device(): lax.psum((grad_first_gain, grad_first_shift, grad_out_bias, grad_second_g...]
where the time goes in v1:
time: 1610 us; the launch traced here: 1600 us
  waiting for transfers between devices  1050 us (65%)
  matrix products  270 us (17%)
  other arithmetic  112 us (7%)
  local copies, waits for them, and re-layouts  93.3 us (6%)
  blocking collectives  57.7 us (4%)
    psum x1, waiting for transfers between devices, on_device(): lax.psum(grad_qkv_weight.astype(jnp.bfloat16), 'dp').astype(jnp.float32)  186 us
    all_gather x1, waiting for transfers between devices, on_device(): normed_first = lax.all_gather(normed_local, 'tensor', axis=0, tiled=True)  130 us
    all_gather x1, waiting for transfers between devices, on_device(): lax.all_gather((unit_second * second_gain + second_shift).astype(jnp.bflo...  125 us
    reduce_scatter x1, waiting for transfers between devices, on_device(): lax.psum_scatter(jnp.einsum('isf,fd->isd', piece, down_weight, preferred_...  123 us
    reduce_scatter x1, waiting for transfers between devices, on_device(): lax.psum_scatter(jnp.einsum('isc,cd->isd', piece, out_weight, preferred_e...  121 us
    reduce_scatter x1, waiting for transfers between devices, on_device(): lax.psum_scatter(jnp.einsum('isf,df->isd', piece, up_weight, preferred_el...  121 us
    reduce_scatter x1, waiting for transfers between devices, on_device(): lax.psum_scatter(jnp.einsum('nisc,ndc->isd', piece, qkv_weight, preferred...  103 us
    all_gather x1, waiting for transfers between devices, on_device(): seed_rows = lax.all_gather(cotangent, 'tensor', axis=0, tiled=True)  99.3 us
  transfers between devices with their start and end apart: 9, of which 9 were waited for; matrix products, arithmetic and copies ran while one was open for 12% of the time, Pallas kernels for 0%

profile of v1, /device:TPU:0, one launch (start us, length us, event | category | flops | bytes accessed | tf_op | source)
XLA Modules:
  0.0 1597.8 jit_solution(7733901305608278045)
XLA Ops:
  14.7 130.0 %all-gather.5.cloned.1.call-done = bf16[8,257,1664]{2,1,0:T(8,128)(2,1)} async-done(((bf16[2,257,1664]{2,1,0:T(8,128)(2,1)}), bf16[8,257,1664]{2,1,0:T(8,128)(2,1)}) %all-gather.5.cloned.1.call-update) | async-done | bytes 6842384 | tf_op jit(solution)/shard_map/all_gather | solution.py:85
  144.7 15.5 convolution_bitcast_fusion
  196.2 24.4 %while.26 = (s32[]{:T(128)}, bf16[4,2,257,4,104]{4,2,3,1,0:T(8,128)(2,1)}, f32[4,2,4,257]{3,2,1,0:T(4,128)}, bf16[4,2,257,4,104]{4,2,3,1,0:T(8,128)(2,1)}, bf16[...) while((s32[]{:T(128)}, bf16[4,2,257,4,104]{4,2,3,1,0:T(8,128)(2,1)}, ...), condition=%wide.region_5.6_spmd, body=%wide.region_2.5_spmd.sunk | while | flops 224564544 | bytes 9116557 | solution.py:97
  237.1 121.2 %reduce-scatter.5.cloned.1.call-done = bf16[2,257,1664]{2,1,0:T(8,128)(2,1)} async-done(((bf16[8,257,1664]{2,1,0:T(8,128)(2,1)}), bf16[2,257,1664]{2,1,0:T(8,128)(2,1)}) %reduce-scatter.5.cloned.1.call-update) | async-done | bytes 1710608 | tf_op jit(solution)/shard_map/reduce_scatter | solution.py:103
  366.6 125.1 %all-gather.7.cloned.1.call-done = bf16[8,257,1664]{2,1,0:T(8,128)(2,1)} async-done(((bf16[2,257,1664]{2,1,0:T(8,128)(2,1)}), bf16[8,257,1664]{2,1,0:T(8,128)(2,1)}) %all-gather.7.cloned.1.call-update) | async-done | bytes 6842384 | tf_op jit(solution)/shard_map/all_gather | solution.py:113
  491.7 28.5 %fusion.91 = (u8[257,2048]{1,0:T(8,128)(4,1)}, u8[257,2048]{1,0:T(8,128)(4,1)}, f32[8,257,2048]{2,1,0:T(8,128)}) fusion(f32[2048]{0:T(1024)S(1)} %copy-done.39, bf16[8,257,1664]{2,1,0:T(8,128)(2,1)} %all-gather.7.cloned.1.call-done, bf16[1664,2048]{1,0:T(8,128)(2,1)} %param.27), kind=kOutput, calls=%fused_computation.123 | convolution fusion | flops 14071066624 | bytes 31561728 | tf_op jit(solution)/shard_map/isd,df->isf/dot_general | solution.py:120
  520.2 99.3 %all-gather.9.cloned.1.call-done = bf16[8,257,1664]{2,1,0:T(8,128)(2,1)} async-done(((bf16[2,257,1664]{2,1,0:T(8,128)(2,1)}), bf16[8,257,1664]{2,1,0:T(8,128)(2,1)}) %all-gather.9.cloned.1.call-update) | async-done | bytes 6842384 | tf_op jit(solution)/shard_map/all_gather | solution.py:137
  619.5 29.1 %fusion.123 = (bf16[2048]{0:T(1024)(128)(2,1)}, bf16[8,257,2048]{2,1,0:T(8,128)(2,1)S(1)}) fusion(f32[8,257,2048]{2,1,0:T(8,128)} %get-tuple-element.259, f32[2048]{0:T(1024)S(1)} %copy-done.39, bf16[8,257,1664]{2,1,0:T(8,128)(2,1)} %all-gather.9.cloned.1.call-done, bf16[2048,1664]{1,0:T(8,128)(2,1)} %param.29), kind=kOutput, calls=%fused_computation.175 | convolution fusion | flops 14063695872 | bytes 38934528 | tf_op jit(solution)/shard_map/isd,fd->isf/dot_general | solution.py:142
  652.0 21.0 %fusion.78 = bf16[8,257,1664]{2,1,0:T(8,128)(2,1)} fusion(bf16[8,257,2048]{2,1,0:T(8,128)(2,1)S(1)} %get-tuple-element.261, bf16[1664,2048]{1,0:T(8,128)(2,1)} %param.27), kind=kOutput, calls=%fused_computation.102 | convolution fusion | flops 14016590848 | bytes 22079488 | tf_op jit(solution)/shard_map/isf,df->isd/dot_general | solution.py:154
  673.1 121.2 %reduce-scatter.9.cloned.1.call-done = bf16[2,257,1664]{2,1,0:T(8,128)(2,1)} async-done(((bf16[8,257,1664]{2,1,0:T(8,128)(2,1)}), bf16[2,257,1664]{2,1,0:T(8,128)(2,1)}) %reduce-scatter.9.cloned.1.call-update) | async-done | bytes 1710608 | tf_op jit(solution)/shard_map/reduce_scatter | solution.py:153
  802.9 42.3 %fusion.52 = bf16[8,257,2048]{2,1,0:T(8,128)(2,1)S(1)} fusion(f32[8,257,2048]{2,1,0:T(8,128)} %get-tuple-element.259, f32[2048]{0:T(1024)S(1)} %copy-done.39, u8[257,2048]{1,0:T(8,128)(4,1)} %get-tuple-element.189, u8[257,2048]{1,0:T(8,128)(4,1)} %get-tuple-element.188), kind=kLoop, calls=%fused_computation.60 | loop fusion | flops 298958848 | bytes 26324992 | tf_op jit(solution)/shard_map/convert_element_type | solution.py:123
  845.2 25.8 %bitcast_convert_fusion.1 = bf16[2048,1664]{1,0:T(8,128)(2,1)} fusion(bf16[8,257,2048]{2,1,0:T(8,128)(2,1)S(1)} %fusion.52, bf16[8,257,1664]{2,1,0:T(8,128)(2,1)} %all-gather.9.cloned.1.call-done), kind=kOutput, calls=%fused_computation.86 | convolution fusion | flops 14016577536 | bytes 22079488 | tf_op jit(solution)/shard_map/isf,isd->fd/dot_general | solution.py:138
  871.1 18.5 %bitcast_convert_fusion.2 = bf16[1664,2048]{1,0:T(8,128)(2,1)} fusion(bf16[8,257,1664]{2,1,0:T(8,128)(2,1)S(1)} %bitcast.177, bf16[8,257,2048]{2,1,0:T(8,128)(2,1)S(1)} %bitcast.179), kind=kOutput, calls=%fused_computation.87 | convolution fusion | flops 14016577536 | bytes 22079488 | tf_op jit(solution)/shard_map/isd,isf->df/dot_general | solution.py:148
  889.5 41.3 %all-gather.11.cloned.1.call-done = bf16[8,257,1664]{2,1,0:T(8,128)(2,1)} async-done(((bf16[2,257,1664]{2,1,0:T(8,128)(2,1)}), bf16[8,257,1664]{2,1,0:T(8,128)(2,1)}) %all-gather.11.cloned.1.call-update) | async-done | bytes 6842384 | tf_op jit(solution)/shard_map/all_gather | solution.py:168
  944.1 50.2 %while.27 = (s32[]{:T(128)}, bf16[4,2,257,4,104]{4,2,3,1,0:T(8,128)(2,1)}, bf16[4,2,257,4,104]{4,3,2,1,0:T(4,128)(2,1)}, bf16[4,2,257,4,104]{4,2,3,1,0:T(8,128)(...) while((s32[]{:T(128)}, ...), condition=%wide.region_15.16_spmd, body=%wide.region_13.15_spmd.sunk | while | flops 556935424 | bytes 23355692 | solution.py:175
  1026.4 15.7 fusion.98
  1042.1 15.3 bitcast_convert_fusion
  1057.5 21.5 %fusion.81 = bf16[8,257,1664]{2,1,0:T(8,128)(2,1)} fusion(bf16[8,257,2048]{2,1,0:T(8,128)(2,1)} %copy-done.9, bf16[2048,1664]{1,0:T(8,128)(2,1)} %param.29), kind=kOutput, calls=%fused_computation.103 | convolution fusion | flops 14016590848 | bytes 22079488 | tf_op jit(solution)/shard_map/isf,fd->isd/dot_general | solution.py:128
  1083.4 15.5 all-reduce.2
  1100.1 186.1 %all-reduce.6.cloned.1.call-done = (bf16[3,1664,416]{1,2,0:T(8,128)(2,1)}, bf16[416,1664]{1,0:T(8,128)(2,1)}, bf16[1664,2048]{1,0:T(8,128)(2,1)}, bf16[2048,1664]{1,0:T(8,128)(2,1)}) async-done(((bf16[3,1664,416]{1,2,0:T(8,128)(2,1)}, bf16[416,1664]{1,0:T(8,128)(2,1)}, bf16[1664,2048]{1,0:T(8,128)(2,1)}, bf16[2048,1664]{1,0:T(8,128)(2,1)}), (bf16[3,1664,416]{1,2,0:T(8,128)(2,1)}, ...) | async-done | bytes 19169296 | tf_op jit(solution)/shard_map/psum | solution.py:217
  1308.5 102.9 %reduce-scatter.11.cloned.1.call-done = bf16[2,257,1664]{2,1,0:T(8,128)(2,1)} async-done(((bf16[8,257,1664]{2,1,0:T(8,128)(2,1)}), bf16[2,257,1664]{2,1,0:T(8,128)(2,1)}) %reduce-scatter.11.cloned.1.call-update) | async-done | bytes 1710608 | tf_op jit(solution)/shard_map/reduce_scatter | solution.py:196
  1414.4 122.8 %reduce-scatter.7.cloned.1.call-done = bf16[2,257,1664]{2,1,0:T(8,128)(2,1)} async-done(((bf16[8,257,1664]{2,1,0:T(8,128)(2,1)}), bf16[2,257,1664]{2,1,0:T(8,128)(2,1)}) %reduce-scatter.7.cloned.1.call-update) | async-done | bytes 1710608 | tf_op jit(solution)/shard_map/reduce_scatter | solution.py:127
  1548.8 18.7 %all-reduce.1 = (f32[1664]{0:T(1024)S(1)}, f32[1664]{0:T(1024)S(1)}, f32[1664]{0:T(1024)S(1)}, f32[1664]{0:T(1024)S(1)}, f32[1664]{0:T(1024)S(1)}, /*index=5*/f32[1664]{0:T(1024)S(1)}) all-reduce(f32[1664]{0:T(1024)S(1)} %get-tuple-element.192, f32[1664]{0:T(1024)S(1)} %get-tuple-element.197, ...), channel_id=1, replica_groups=mesh['dp'=8,'tensor'=4] {'tensor'}, use_global_device_ids=true, to_apply=%region_20.21 | all-reduce | flops 9984 | bytes 79872 | tf_op jit(solution)/shard_map/psum | solution.py:232
  1567.5 23.5 %all-reduce = (f32[1664]{0:T(1024)}, f32[1664]{0:T(1024)}, f32[1664]{0:T(1024)}, f32[1664]{0:T(1024)}, f32[1664]{0:T(1024)}, /*index=5*/f32[1664]{0:T(1024)}) all-reduce(f32[1664]{0:T(1024)S(1)} %get-tuple-element.236, f32[1664]{0:T(1024)S(1)} %get-tuple-element.237, ...), channel_id=1, replica_groups=mesh['dp'=8,'tensor'=4] {'dp'}, use_global_device_ids=true, to_apply=%region_21.22 | all-reduce | flops 9984 | bytes 79872 | tf_op jit(solution)/shard_map/psum | solution.py:231
  (233 shorter events, 242.2 us)
Async XLA Ops:
  7.2 221.7 %copy-start = (bf16[416,1664]{1,0:T(8,128)(2,1)S(1)}, bf16[416,1664]{1,0:T(8,128)(2,1)}, u32[]{:S(2)}) copy-start(bf16[416,1664]{1,0:T(8,128)(2,1)} %param.23) | copy-start | bytes 4153348
  7.2 137.5 %all-gather.5.cloned.1.call-start = ((), (), s32[]{:S(2)}) async-start(), calls=%async_computation.4 | async-start | bytes 8785920 | tf_op jit(solution)/shard_map/all_gather | solution.py:85
  14.5 343.9 %reduce-scatter.5.cloned.1.call-start = ((), (), s32[]{:S(2)}) async-start(), calls=%async_computation.5 | async-start | bytes 8785920 | tf_op jit(solution)/shard_map/reduce_scatter | solution.py:103
  237.0 121.3 %copy-start.17 = (f32[1664]{0:T(1024)S(1)}, f32[1664]{0:T(1024)}, u32[]{:S(2)}) copy-start(f32[1664]{0:T(1024)} %param.24) | copy-start | bytes 19972
  237.1 124.4 %copy-start.19 = (f32[1664]{0:T(1024)S(1)}, f32[1664]{0:T(1024)}, u32[]{:S(2)}) copy-start(f32[1664]{0:T(1024)} %param.25) | copy-start | bytes 19972
  237.1 124.4 %copy-start.38 = (f32[1664]{0:T(1024)S(1)}, f32[1664]{0:T(1024)}, u32[]{:S(2)}) copy-start(f32[1664]{0:T(1024)} %param.26) | copy-start | bytes 19972
  237.1 254.6 %all-gather.7.cloned.1.call-start = ((), (), s32[]{:S(2)}) async-start(), calls=%async_computation.6 | async-start | bytes 8785920 | tf_op jit(solution)/shard_map/all_gather | solution.py:113
  360.5 438.2 %copy-start.21 = (f32[2,257]{1,0:T(2,128)}, f32[2,257]{1,0:T(2,128)S(1)}, u32[]{:S(2)}) copy-start(f32[2,257]{1,0:T(2,128)S(1)} %broadcast_multiply_fusion.4) | copy-start | bytes 6172
  361.5 437.2 %copy-start.23 = (f32[2,257]{1,0:T(2,128)}, f32[2,257]{1,0:T(2,128)S(1)}, u32[]{:S(2)}) copy-start(f32[2,257]{1,0:T(2,128)S(1)} %add_rsqrt_fusion) | copy-start | bytes 6172
  363.6 128.1 %copy-start.39 = (f32[2048]{0:T(1024)S(1)}, f32[2048]{0:T(1024)}, u32[]{:S(2)}) copy-start(f32[2048]{0:T(1024)} %param.28) | copy-start | bytes 24580
  363.7 255.8 %all-gather.9.cloned.1.call-start = ((), (), s32[]{:S(2)}) async-start(), calls=%async_computation.8 | async-start | bytes 8785920 | tf_op jit(solution)/shard_map/all_gather | solution.py:137
  366.6 427.7 %reduce-scatter.9.cloned.1.call-start = ((), (), s32[]{:S(2)}) async-start(), calls=%async_computation.9 | async-start | bytes 8785920 | tf_op jit(solution)/shard_map/reduce_scatter | solution.py:153
  673.1 257.8 %all-gather.11.cloned.1.call-start = ((), (), s32[]{:S(2)}) async-start(), calls=%async_computation.10 | async-start | bytes 8785920 | tf_op jit(solution)/shard_map/all_gather | solution.py:168
  802.8 483.4 %all-reduce.6.cloned.1.call-start = ((), (), s32[]{:S(2)}) async-start(), calls=%async_computation.12 | async-start | bytes 38338560 | tf_op jit(solution)/shard_map/psum | solution.py:217
  1042.1 369.3 %reduce-scatter.11.cloned.1.call-start = ((), (), s32[]{:S(2)}) async-start(), calls=%async_computation.11 | async-start | bytes 8785920 | tf_op jit(solution)/shard_map/reduce_scatter | solution.py:196
  1057.5 479.8 %reduce-scatter.7.cloned.1.call-start = ((), (), s32[]{:S(2)}) async-start(), calls=%async_computation.7 | async-start | bytes 8785920 | tf_op jit(solution)/shard_map/reduce_scatter | solution.py:127
  1306.7 104.7 %copy-start.29 = (f32[2,257]{1,0:T(2,128)S(1)}, f32[2,257]{1,0:T(2,128)}, u32[]{:S(2)}) copy-start(f32[2,257]{1,0:T(2,128)} %copy-done.28) | copy-start | bytes 6172
  1306.7 230.6 %copy-start.18 = (f32[1664]{0:T(1024)S(1)}, f32[1664]{0:T(1024)}, u32[]{:S(2)}) copy-start(f32[1664]{0:T(1024)} %param.24) | copy-start | bytes 19972
  1306.7 230.6 %copy-start.20 = (f32[1664]{0:T(1024)S(1)}, f32[1664]{0:T(1024)}, u32[]{:S(2)}) copy-start(f32[1664]{0:T(1024)} %param.25) | copy-start | bytes 19972
  1306.7 230.5 %copy-start.22 = (f32[2,257]{1,0:T(2,128)S(1)}, f32[2,257]{1,0:T(2,128)}, u32[]{:S(2)}) copy-start(f32[2,257]{1,0:T(2,128)} %copy-done.21) | copy-start | bytes 6172
  1306.7 230.5 %copy-start.24 = (f32[2,257]{1,0:T(2,128)S(1)}, f32[2,257]{1,0:T(2,128)}, u32[]{:S(2)}) copy-start(f32[2,257]{1,0:T(2,128)} %copy-done.23) | copy-start | bytes 6172
  1306.7 230.5 %copy-start.35 = (f32[2,257]{1,0:T(2,128)S(1)}, f32[2,257]{1,0:T(2,128)}, u32[]{:S(2)}) copy-start(f32[2,257]{1,0:T(2,128)} %copy-done.34) | copy-start | bytes 6172
  1306.7 230.5 %copy-start.37 = (f32[2,257]{1,0:T(2,128)S(1)}, f32[2,257]{1,0:T(2,128)}, u32[]{:S(2)}) copy-start(f32[2,257]{1,0:T(2,128)} %copy-done.36) | copy-start | bytes 6172
  1306.8 230.5 %copy-start.40 = (f32[1664]{0:T(1024)S(1)}, f32[1664]{0:T(1024)}, u32[]{:S(2)}) copy-start(f32[1664]{0:T(1024)} %param.30) | copy-start | bytes 19972
  (34 other events, 705.2 us)
Sparse Core Ops, SparseCore 0:
  14.6 130.0 all-gather.4
  237.2 121.1 reduce-scatter.4
  363.8 127.9 all-gather.6
  493.8 125.6 all-gather.8
  673.2 121.0 reduce-scatter.8
  802.9 127.9 all-gather.10
  1042.2 243.9 all-reduce.5
  1288.5 122.8 reduce-scatter.10
  1413.8 123.3 reduce-scatter.6
